TPU v7x, 512 devices: a whole 4x8x8 slice. The times are simulated.
512 devices in a mesh: row: 16 (over y_hi, x), pair: 32 (over y_lo, z, core).
Axes of the slice: x: 4, y: 8 (y_hi: 4, y_lo: 2; y = y_hi * 2 + y_lo), z: 8, core: 2. Of those that a mesh axis runs over, the one named last changes fastest.
Arguments:
- embedding: float32 [32768, 8192], P(('row', 'pair')), may hold values from -54 to 54
- pairing: int32 [64], replicated, may hold values from 0 to 63, each once
Outputs:
- rotated: float32 [32768, 8192], P('row', 'pair')
Inputs may be any that keep to these rules, and one draw needn't show every extreme that they name: `pairing`: each column block index from 0 to 63 appears exactly once.
All inputs are finite; a program needn't handle non-finite values.
Results may differ from a plain program's by a relative error of at most 0.0003.
Values sent between devices are 32-bit elements; how exact they have to be, the bound alone decides.
A program may use at most 64 MiB of HBM per device.

v0:
```python
import functools

import jax
import jax.numpy as jnp
from jax import lax
from jax.experimental import pallas as pl
from jax.experimental.pallas import tpu as pltpu
from jax.sharding import PartitionSpec as P

ROUNDS = 3
SWEEPS = 2
F32 = jnp.float32
BF16 = jnp.bfloat16


def halves(a):
    high = a.astype(BF16)
    return high, (a - high.astype(F32)).astype(BF16)


def product(a, b, dims=((1,), (0,))):
    def one(x, y):
        return lax.dot_general(x, y, (dims, ((), ())), preferred_element_type=F32)

    a_high, a_low = a
    b_high, b_low = b
    return one(a_high, b_high) + (one(a_high, b_low) + one(a_low, b_high))


def rotation_kernel(total_rows, gram_ref, rotation_ref, upper_ref, lower_ref, current, basis, level, strict):
    width = gram_ref.shape[0]
    block = width // 2
    rows = lax.broadcasted_iota(jnp.int32, (width, width), 0)
    cols = lax.broadcasted_iota(jnp.int32, (width, width), 1)
    eye = rows == cols
    above = rows < cols

    def diag_row(a):
        return jnp.sum(jnp.where(eye, a, 0.0), axis=0, keepdims=True)

    def diag_col(a):
        return jnp.sum(jnp.where(eye, a, 0.0), axis=1, keepdims=True)

    current[...] = gram_ref[...]
    for sweep in range(SWEEPS):
        scaled = current[...] * (1.0 / total_rows)
        level_row = diag_row(scaled) + 1e-06
        level_col = diag_col(scaled) + 1e-06
        spread = level_row - level_col
        generator = scaled * spread / (spread * spread + 0.25 * level_col * level_row)
        parts = halves(generator)
        square = product(parts, parts)
        basis[...] = jnp.where(eye, 1.0, 0.0) + generator
        level[...] = 1.0 - diag_col(square)
        strict[...] = jnp.where(above, -square, 0.0)
        size = jnp.sum(square * square * jnp.where(above, 1.0, 0.0))

        @pl.when(size > 0.0625)
        def _():
            exact = jnp.dot(generator, generator, precision=lax.Precision.HIGHEST, preferred_element_type=F32)
            current_metric = jnp.where(eye, 1.0, 0.0) - exact
            strict[...] = 0.5 * (current_metric + current_metric.T)

            def step(k, _):
                pivot_row = strict[pl.ds(k, 1), :]
                lane = lax.broadcasted_iota(jnp.int32, (1, width), 1)
                pivot = jnp.sum(jnp.where(lane == k, pivot_row, 0.0), axis=1, keepdims=True)
                after = jnp.where(lane > k, pivot_row / pivot, 0.0)
                metric = strict[...]
                pivot_col = jnp.sum(jnp.where(cols == k, metric, 0.0), axis=1, keepdims=True)
                strict[...] = metric - pivot_col * after
                turned = basis[...]
                basis_col = jnp.sum(jnp.where(cols == k, turned, 0.0), axis=1, keepdims=True)
                basis[...] = turned - basis_col * after
                return 0

            lax.fori_loop(0, width, step, 0)
            level[...] = diag_col(strict[...])
            strict[...] = jnp.zeros_like(strict)

        def eliminate(state):
            _, count = state
            upper = strict[...]
            scale = level[...]
            ratio = upper / scale
            ratio_parts = halves(ratio)
            turned = basis[...]
            basis[...] = turned - product(halves(turned), ratio_parts)
            size_now = jnp.sum(upper * upper)

            @pl.when(size_now > 1e-06)
            def _():
                second = product(halves(upper), ratio_parts)
                mixed = product(halves(ratio.T), halves(0.5 * upper - second))
                level[...] = scale - 2.0 * diag_col(mixed)
                strict[...] = jnp.where(above, -(second + mixed + mixed.T), 0.0)

            return size_now, count + 1

        lax.while_loop(
            lambda state: jnp.logical_and(state[0] > 1e-06, state[1] < width),
            eliminate,
            (jnp.float32(1.0), jnp.int32(0)),
        )
        level_out = jnp.sum(jnp.where(eye, jnp.broadcast_to(level[...], (width, width)), 0.0), axis=0, keepdims=True)
        step_rot = basis[...] * lax.rsqrt(level_out)
        step_parts = halves(step_rot)
        half = product(halves(current[...]), step_parts)
        if sweep == 0:
            rotation_ref[...] = step_rot
        else:
            rotation_ref[...] = product(halves(rotation_ref[...]), step_parts)
        if sweep + 1 < SWEEPS:
            current[...] = product(halves(step_rot.T), halves(half))
        else:
            turned_t = step_rot.T
            upper_ref[...] = product(halves(turned_t[:block]), halves(half[:, :block]))
            lower_ref[...] = product(halves(turned_t[block:]), halves(half[:, block:]))


def make_rotation(gram, total_rows):
    width = gram.shape[0]
    block = width // 2
    return pl.pallas_call(
        functools.partial(rotation_kernel, total_rows),
        out_shape=(
            jax.ShapeDtypeStruct((width, width), F32),
            jax.ShapeDtypeStruct((block, block), F32),
            jax.ShapeDtypeStruct((block, block), F32),
        ),
        in_specs=[pl.BlockSpec(memory_space=pltpu.VMEM)],
        out_specs=(pl.BlockSpec(memory_space=pltpu.VMEM),) * 3,
        scratch_shapes=[
            pltpu.VMEM((width, width), F32),
            pltpu.VMEM((width, width), F32),
            pltpu.VMEM((width, 1), F32),
            pltpu.VMEM((width, width), F32),
        ],
        compiler_params=pltpu.CompilerParams(vmem_limit_bytes=14 * 2**20),
        name="rotation",
    )(gram)


MESH = pl.DeviceIdType.MESH
CHUNK = 256
GRAM_STREAMS = 3
CROSS_STREAMS = 2
DEAL_AHEAD = 5
ROUND_AHEAD = 3
GRANT = 20 * 2**20


def greet(peers):
    barrier = pltpu.get_barrier_semaphore()
    for peer, wanted in peers:
        if wanted is None:
            pl.semaphore_signal(barrier, inc=1, device_id=peer, device_id_type=MESH)
        else:

            @pl.when(wanted)
            def _(peer=peer):
                pl.semaphore_signal(barrier, inc=1, device_id=peer, device_id_type=MESH)


def met(count):
    pl.semaphore_wait(pltpu.get_barrier_semaphore(), count)


def row_place(grid):
    deep, wide = grid
    me = lax.axis_index("row")
    return me // wide, me % wide


def row_peers(grid):
    deep, wide = grid
    down, across = row_place(grid)
    peers = [({"row": down * wide + (across + j) % wide}, None) for j in range(1, wide)]
    return peers + [({"row": partner * wide + across}, None) for partner in y_partners(deep, down)]


def y_partners(deep, down):
    assert deep == 4
    return down + 1 - 2 * (down % 2), deep - 1 - down


def row_total(grid, streams, part, total, slots, sums, send, recv, beside):
    deep, wide = grid
    down, across = row_place(grid)
    piece = part.shape[0] // (wide * streams)

    def rows_of(stream, owner):
        return pl.ds(pl.multiple_of((stream * wide + owner) * piece, 8), piece)

    def across_peer(j):
        return {"row": down * wide + (across + j) % wide}

    def scatter(stream, j):
        theirs = rows_of(stream, (across + j) % wide)
        return pltpu.make_async_remote_copy(
            part.at[theirs], slots.at[stream, j], send.at[0, stream, j], recv.at[0, stream, j], across_peer(j), MESH
        )

    def exchange(stream, step):
        peer = {"row": y_partners(deep, down)[step] * wide + across}
        return pltpu.make_async_remote_copy(
            sums.at[stream, 2 * step], sums.at[stream, 2 * step + 1], send.at[1, stream, step],
            recv.at[1, stream, step], peer, MESH,
        )

    def gather(stream, j):
        mine = total.at[rows_of(stream, across)]
        return pltpu.make_async_remote_copy(
            mine, mine, send.at[2, stream, j], recv.at[2, stream, j], across_peer(j), MESH
        )

    for stream in range(streams):
        for j in range(1, wide):
            scatter(stream, j).start()
    beside(0)
    for stream in range(streams):
        for j in range(1, wide):
            scatter(stream, j).wait_recv()
        value = part[rows_of(stream, across), :]
        for j in range(1, wide):
            value = value + slots[stream, j]
        sums[stream, 0] = value
        exchange(stream, 0).start()
    beside(1)
    for stream in range(streams):
        exchange(stream, 0).wait_recv()
        sums[stream, 2] = sums[stream, 0] + sums[stream, 1]
        exchange(stream, 1).start()
    beside(2)
    for stream in range(streams):
        exchange(stream, 1).wait_recv()
        value = sums[stream, 2] + sums[stream, 3]
        total[rows_of(stream, across), :] = value
        for j in range(1, wide):
            gather(stream, j).start()
    for stream in range(streams):
        for j in range(1, wide):
            gather(stream, j).wait_recv()
    for stream in range(streams):
        for j in range(1, wide):
            scatter(stream, j).wait_send()
            gather(stream, j).wait_send()
        for step in range(2):
            exchange(stream, step).wait_send()


def total_scratch(grid, streams, rows, block):
    deep, wide = grid
    steps = max(grid)
    piece = rows // (wide * streams)
    return [
        pltpu.VMEM((rows, block), F32),
        pltpu.VMEM((rows, block), F32),
        pltpu.VMEM((streams, wide, piece, block), F32),
        pltpu.VMEM((streams, 4, piece, block), F32),
        pltpu.SemaphoreType.DMA((3, streams, steps)),
        pltpu.SemaphoreType.DMA((3, streams, steps)),
    ]


def chunk_rows(c):
    return pl.ds(pl.multiple_of(c * CHUNK, CHUNK), CHUNK)


def both_ways(onward, backward, first, last, act):
    @pl.when(jnp.logical_not(last))
    def _():
        act(onward)

    @pl.when(jnp.logical_not(first))
    def _():
        act(backward)


def both_arrive(onward, backward, first, last):
    @pl.when(jnp.logical_not(first))
    def _():
        onward.wait_recv()

    @pl.when(jnp.logical_not(last))
    def _():
        backward.wait_recv()


def neighbour_copies(sources, targets, sends, recvs, position):
    def one(way, distance):
        return pltpu.make_async_remote_copy(
            sources[way], targets[way], sends[way], recvs[way], {"pair": position + distance}, MESH
        )

    return one(0, 1), one(1, -1)


def raw_moves(blocks, before, after, send, recv, position, first, last, span):
    pieces = 2 * (before.shape[1] // CHUNK)

    def copies(k):
        half = k % 2
        rows = chunk_rows(k // 2)
        source = blocks.at[half, rows]
        return neighbour_copies(
            (source, source),
            (before.at[half, rows], after.at[half, rows]),
            (send.at[0, k], send.at[1, k]),
            (recv.at[0, k], recv.at[1, k]),
            position,
        )

    bent_on = (position + 1) % span == 0
    bent_back = position % span == 0
    cuts_at = (0, (pieces + 1) // 3, (2 * pieces + 1) // 3, pieces)

    def start(low, high, on, back):
        def one(k, _):
            onward, backward = copies(k)

            @pl.when(jnp.logical_and(jnp.logical_not(last), on))
            def _():
                onward.start()

            @pl.when(jnp.logical_and(jnp.logical_not(first), back))
            def _():
                backward.start()

            return 0

        lax.fori_loop(low, high, one, 0)

    def beside(phase):
        if phase == 0:
            start(0, pieces, jnp.logical_not(bent_on), jnp.logical_not(bent_back))
        start(cuts_at[phase], cuts_at[phase + 1], bent_on, bent_back)

    def finish():
        def one(k, _):
            both_arrive(*copies(k), first, last)
            both_ways(*copies(k), first, last, lambda copy: copy.wait_send())
            return 0

        lax.fori_loop(0, pieces, one, 0)

    return beside, finish


def turn_and_move(
    blocks, before, after, rotation, fresh, ahead, back, own_high, own_low, lent, got, got_high, got_low,
    send, recv, spin_send, spin_recv, first, last, position, count, use,
):
    block = blocks.shape[2]
    chunks = blocks.shape[1] // CHUNK
    there = before.shape[1] // CHUNK
    high, low = halves(rotation[...])
    own_high[...] = high
    own_low[...] = low
    lent[0] = jnp.where(first, rotation[:, block:], rotation[:, :block])
    lent[1] = rotation[:, block:]

    def pair_rows(source, c):
        rows = chunk_rows(c)
        return halves(jnp.concatenate([source[0, rows, :], source[1, rows, :]], axis=1))

    def copies(c):
        rows = chunk_rows(c)
        return neighbour_copies(
            (ahead.at[rows], back.at[rows]),
            (fresh.at[0, rows], fresh.at[1, rows]),
            (send.at[0, c], send.at[1, c]),
            (recv.at[0, c], recv.at[1, c]),
            position,
        )

    def spins():
        return neighbour_copies(
            (lent.at[0], lent.at[1]),
            (got.at[0], got.at[1]),
            (spin_send.at[0], spin_send.at[1]),
            (spin_recv.at[0], spin_recv.at[1]),
            position,
        )

    def turn(c, _):
        rows = chunk_rows(c)
        turned = product(pair_rows(blocks, c), (own_high[...], own_low[...]))
        upper, lower = turned[:, :block], turned[:, block:]
        ahead[rows, :] = jnp.where(first, lower, upper)
        back[rows, :] = lower

        @pl.when(first)
        def _():
            fresh[0, rows, :] = upper

        @pl.when(last)
        def _():
            fresh[1, rows, :] = upper

        return 0

    def leave(c, _):
        both_ways(*copies(c), first, last, lambda copy: copy.start())
        return 0

    def turn_and_leave(c, _):
        turn(c, 0)
        return leave(c, 0)

    early = (chunks + there) // 2
    lax.fori_loop(there, early, turn, 0)
    met(count)
    both_ways(*spins(), first, last, lambda copy: copy.start())
    lax.fori_loop(there, early, leave, 0)
    lax.fori_loop(early, chunks, turn_and_leave, 0)
    both_arrive(*spins(), first, last)

    for way, edge in ((0, first), (1, last)):

        @pl.when(edge)
        def _(way=way):
            got_high[way] = own_high[:, :block]
            got_low[way] = own_low[:, :block]

        @pl.when(jnp.logical_not(edge))
        def _(way=way):
            high, low = halves(got[way])
            got_high[way] = high
            got_low[way] = low

    def turn_there(c, _):
        rows = chunk_rows(c)
        for way, edge, raw in ((0, first, before), (1, last, after)):

            @pl.when(edge)
            def _(way=way):
                fresh[way, rows, :] = product(pair_rows(blocks, c), (got_high[way], got_low[way]))

            @pl.when(jnp.logical_not(edge))
            def _(way=way, raw=raw):
                fresh[way, rows, :] = product(pair_rows(raw, c), (got_high[way], got_low[way]))

        use(c)
        return 0

    lax.fori_loop(0, there, turn_there, 0)

    def take():
        def one(c, _):
            both_arrive(*copies(c), first, last)
            use(c)
            return 0

        lax.fori_loop(there, chunks, one, 0)

    def finish():
        both_ways(*spins(), first, last, lambda copy: copy.wait_send())

        def left(c, _):
            both_ways(*copies(c), first, last, lambda copy: copy.wait_send())
            return 0

        lax.fori_loop(there, chunks, left, 0)

    return take, finish


def pair_place():
    position = lax.axis_index("pair")
    first = position == 0
    last = position == lax.axis_size("pair") - 1
    count = jnp.where(first, 0, 1) + jnp.where(last, 0, 1)
    peers = [
        ({"pair": position + 1}, jnp.logical_not(last)),
        ({"pair": position - 1}, jnp.logical_not(first)),
    ]
    return position, first, last, peers, count


def round_kernel(
    grid, span, blocks, before, after, rotation, upper_gram, lower_gram, fresh, gram, next_before, next_after,
    ahead, back, own_high, own_low, lent, got, got_high, got_low, send, recv, spin_send, spin_recv,
    ahead_gram, back_gram, gram_send, gram_recv, raw_send, raw_recv,
    part, total, slots, sums, sum_send, sum_recv,
):
    position, first, last, peers, count = pair_place()
    block = blocks.shape[2]
    across = row_peers(grid)
    greet(peers + across)
    ahead_gram[...] = jnp.where(first, lower_gram[...], upper_gram[...])
    back_gram[...] = lower_gram[...]

    @pl.when(first)
    def _():
        gram[:block, :block] = upper_gram[...]

    @pl.when(last)
    def _():
        gram[block:, block:] = upper_gram[...]

    part[...] = jnp.zeros_like(part)

    def cross(c):
        rows = chunk_rows(c)
        part[...] += product(halves(fresh[0, rows, :]), halves(fresh[1, rows, :]), ((0,), (0,)))

    take, finish = turn_and_move(
        blocks, before, after, rotation, fresh, ahead, back, own_high, own_low, lent, got, got_high, got_low,
        send, recv, spin_send, spin_recv, first, last, position, count + len(across), cross,
    )

    def grams():
        return neighbour_copies(
            (ahead_gram, back_gram),
            (gram.at[pl.ds(0, block), pl.ds(0, block)], gram.at[pl.ds(block, block), pl.ds(block, block)]),
            (gram_send.at[0], gram_send.at[1]),
            (gram_recv.at[0], gram_recv.at[1]),
            position,
        )

    beside, raws_finish = raw_moves(
        fresh, next_before, next_after, raw_send, raw_recv, position, first, last, span
    )
    both_ways(*grams(), first, last, lambda copy: copy.start())
    take()
    row_total(grid, CROSS_STREAMS, part, total, slots, sums, sum_send, sum_recv, beside)
    gram[:block, block:] = total[...]
    gram[block:, :block] = total[...].T
    both_arrive(*grams(), first, last)
    both_ways(*grams(), first, last, lambda copy: copy.wait_send())
    raws_finish()
    finish()


def last_kernel(
    blocks, before, after, rotation, fresh,
    ahead, back, own_high, own_low, lent, got, got_high, got_low, send, recv, spin_send, spin_recv,
):
    position, first, last, peers, count = pair_place()
    greet(peers)
    take, finish = turn_and_move(
        blocks, before, after, rotation, fresh, ahead, back, own_high, own_low, lent, got, got_high, got_low,
        send, recv, spin_send, spin_recv, first, last, position, count, lambda c: None,
    )
    take()
    finish()


def move_scratch(rows, block):
    width = 2 * block
    chunks = rows // CHUNK
    return [
        pltpu.VMEM((rows, block), F32),
        pltpu.VMEM((rows, block), F32),
        pltpu.VMEM((width, width), BF16),
        pltpu.VMEM((width, width), BF16),
        pltpu.VMEM((2, width, block), F32),
        pltpu.VMEM((2, width, block), F32),
        pltpu.VMEM((2, width, block), BF16),
        pltpu.VMEM((2, width, block), BF16),
        pltpu.SemaphoreType.DMA((2, chunks)),
        pltpu.SemaphoreType.DMA((2, chunks)),
        pltpu.SemaphoreType.DMA((2,)),
        pltpu.SemaphoreType.DMA((2,)),
    ]


VMEM = pl.BlockSpec(memory_space=pltpu.VMEM)


def raw_shape(chunks, block):
    return jax.ShapeDtypeStruct((2, chunks * CHUNK, block), F32)


def next_round(blocks, before, after, rotation, upper_gram, lower_gram, grid, span, collective):
    _, rows, block = blocks.shape
    return pl.pallas_call(
        functools.partial(round_kernel, grid, span),
        out_shape=(
            jax.ShapeDtypeStruct(blocks.shape, F32),
            jax.ShapeDtypeStruct((2 * block, 2 * block), F32),
            raw_shape(ROUND_AHEAD, block),
            raw_shape(ROUND_AHEAD, block),
        ),
        in_specs=[VMEM] * 6,
        out_specs=(VMEM,) * 4,
        scratch_shapes=move_scratch(rows, block)
        + [pltpu.VMEM((block, block), F32), pltpu.VMEM((block, block), F32)]
        + [pltpu.SemaphoreType.DMA((2,))] * 2
        + [pltpu.SemaphoreType.DMA((2, 2 * ROUND_AHEAD))] * 2
        + total_scratch(grid, CROSS_STREAMS, block, block),
        compiler_params=pltpu.CompilerParams(
            collective_id=collective, has_side_effects=True, vmem_limit_bytes=GRANT
        ),
        name="next_round",
    )(blocks, before, after, rotation, upper_gram, lower_gram)


def last_round(blocks, before, after, rotation):
    _, rows, block = blocks.shape
    return pl.pallas_call(
        last_kernel,
        out_shape=jax.ShapeDtypeStruct(blocks.shape, F32),
        in_specs=[VMEM] * 4,
        out_specs=VMEM,
        scratch_shapes=move_scratch(rows, block),
        compiler_params=pltpu.CompilerParams(collective_id=1, has_side_effects=True, vmem_limit_bytes=GRANT),
        name="last_round",
    )(blocks, before, after, rotation)


def pick_kernel(embedding, pairing, picked):
    block = picked.shape[3]

    def one(target, _):
        for half in range(2):
            source = pl.multiple_of(pairing[2 * target + half] * block, block)
            picked[target, half] = embedding[:, pl.ds(source, block)]
        return 0

    lax.fori_loop(0, picked.shape[0], one, 0, unroll=4)


def pick(embedding, pairing):
    sub_rows, columns = embedding.shape
    slots = pairing.shape[0]
    return pl.pallas_call(
        pick_kernel,
        out_shape=jax.ShapeDtypeStruct((slots // 2, 2, sub_rows, columns // slots), F32),
        in_specs=[VMEM, pl.BlockSpec(memory_space=pltpu.SMEM)],
        out_specs=VMEM,
        compiler_params=pltpu.CompilerParams(vmem_limit_bytes=GRANT),
        name="pick",
    )(embedding, pairing)


def deal_kernel(
    grid, cut, outgoing, blocks, gram, before, after, send, recv, own, raw_send, raw_recv,
    part, total, slots, sums, sum_send, sum_recv,
):
    tall, ring, cores = cut
    sub_rows = outgoing.shape[2]
    block = blocks.shape[2]
    devices = lax.axis_size("pair")
    me = lax.axis_index("pair")
    core, turn, side = me % cores, me // cores % ring, me // (cores * ring)
    halfway = ring // 2
    group = tall * cores

    def device(there_side, there_turn, there_core):
        return (there_side % tall * ring + (there_turn + 2 * ring) % ring) * cores + there_core % cores

    def target_of(far, near):
        return device(side + near // cores, turn + far, core + near % cores)

    def rows_of(index):
        return pl.ds(pl.multiple_of(index * sub_rows, sub_rows), sub_rows)

    def far_of(order):
        away = (order + 1) // 2
        return halfway + away - 2 * away * (order % 2)

    def copy_at(far, near):
        target = target_of(far, near)
        step = far * group + near
        return pltpu.make_async_remote_copy(
            outgoing.at[target], blocks.at[:, rows_of(me), :], send.at[step], recv.at[step], {"pair": target}, MESH
        )

    barrier = pltpu.get_barrier_semaphore()

    def call(step, _):
        target = target_of(step // group, step % group)
        pl.semaphore_signal(barrier, inc=1, device_id={"pair": target}, device_id_type=MESH)
        return 0

    lax.fori_loop(1, devices, call, 0)
    across = row_peers(grid)
    greet(across)
    keep = pltpu.make_async_copy(outgoing.at[me], blocks.at[:, rows_of(me), :], own)
    keep.start()
    met(devices - 1 + len(across))
    def send_all(order, _):
        for near in range(group):
            copy_at(far_of(order), near).start()
        return 0

    lax.fori_loop(0, ring - 1, send_all, 0)
    for near in range(1, group):
        copy_at(0, near).start()
    keep.wait()
    part[...] = jnp.zeros_like(part)

    def add(order, _):
        far = far_of(order)
        for near in range(group):

            @pl.when(far * group + near > 0)
            def _(near=near):
                copy_at(far, near).wait_recv()

        for there in range(tall):
            source = (there * ring + (turn - far + ring) % ring) * cores
            rows = pl.ds(pl.multiple_of(source * sub_rows, sub_rows * cores), sub_rows * cores)
            high, low = halves(jnp.concatenate([blocks[0, rows, :], blocks[1, rows, :]], axis=1))

            def one(x, y):
                return lax.dot_general(x, y, (((0,), (0,)), ((), ())), preferred_element_type=F32)

            main, side_part = one(high, high), one(high, low)
            whole = main + (side_part + side_part.T)
            part[:block, :] += whole[:block, :block]
            part[block : 2 * block, :] += whole[:block, block:]
            part[2 * block :, :] += whole[block:, block:]
        return 0

    lax.fori_loop(0, ring, add, 0)
    position, first, last, _, _ = pair_place()

    beside, raws_finish = raw_moves(
        blocks, before, after, raw_send, raw_recv, position, first, last, ring * cores
    )
    row_total(grid, GRAM_STREAMS, part, total, slots, sums, sum_send, sum_recv, beside)
    gram[:block, :block] = total[:block, :]
    gram[:block, block:] = total[block : 2 * block, :]
    gram[block:, :block] = total[block : 2 * block, :].T
    gram[block:, block:] = total[2 * block :, :]

    raws_finish()

    def sent(step, _):
        copy_at(step // group, step % group).wait_send()
        return 0

    lax.fori_loop(1, devices, sent, 0)


def deal(picked, grid, cut):
    devices, _, sub_rows, block = picked.shape
    return pl.pallas_call(
        functools.partial(deal_kernel, grid, cut),
        out_shape=(
            jax.ShapeDtypeStruct((2, sub_rows * devices, block), F32),
            jax.ShapeDtypeStruct((2 * block, 2 * block), F32),
            raw_shape(DEAL_AHEAD, block),
            raw_shape(DEAL_AHEAD, block),
        ),
        in_specs=[VMEM],
        out_specs=(VMEM,) * 4,
        scratch_shapes=[
            pltpu.SemaphoreType.DMA((devices,)),
            pltpu.SemaphoreType.DMA((devices,)),
            pltpu.SemaphoreType.DMA,
            pltpu.SemaphoreType.DMA((2, 2 * DEAL_AHEAD)),
            pltpu.SemaphoreType.DMA((2, 2 * DEAL_AHEAD)),
        ]
        + total_scratch(grid, GRAM_STREAMS, 3 * block, block),
        compiler_params=pltpu.CompilerParams(collective_id=0, has_side_effects=True, vmem_limit_bytes=GRANT),
        name="deal",
    )(picked)


def join_kernel(blocks, joined, sems):
    block = blocks.shape[2]
    parts = sems.shape[1]
    rows = blocks.shape[1] // parts
    copies = []
    for half in range(2):
        for part in range(parts):
            here = pl.ds(part * rows, rows)
            copies.append(
                pltpu.make_async_copy(
                    blocks.at[half, here], joined.at[here, pl.ds(half * block, block)], sems.at[half, part]
                )
            )
            copies[-1].start()
    for copy in copies:
        copy.wait()


def join(blocks):
    _, rows, block = blocks.shape
    return pl.pallas_call(
        join_kernel,
        out_shape=jax.ShapeDtypeStruct((rows, 2 * block), F32),
        in_specs=[pl.BlockSpec(memory_space=pl.ANY)],
        out_specs=pl.BlockSpec(memory_space=pltpu.HBM),
        scratch_shapes=[pltpu.SemaphoreType.DMA((2, 4))],
        compiler_params=pltpu.CompilerParams(vmem_limit_bytes=GRANT),
        name="join",
    )(blocks)


def cuts():
    grids = {16: (4, 4), 4: (2, 2)}
    pairs = {32: (2, 8, 2), 4: (1, 2, 2)}
    return grids[lax.axis_size("row")], pairs[lax.axis_size("pair")]


def body(embedding, pairing):
    grid, cut = cuts()
    blocks, gram, before, after = deal(pick(embedding, pairing), grid, cut)
    total_rows = blocks.shape[1] * lax.axis_size("row")
    for round_num in range(ROUNDS):
        rotation, upper_gram, lower_gram = make_rotation(gram, total_rows)
        if round_num + 1 < ROUNDS:
            blocks, gram, before, after = next_round(
                blocks, before, after, rotation, upper_gram, lower_gram, grid, cut[1] * cut[2], 2 + round_num
            )
        else:
            blocks = last_round(blocks, before, after, rotation)
    return join(blocks)


def solution(mesh):
    in_specs = (P(("row", "pair"), None), P())
    out_specs = P("row", "pair")
    return jax.shard_map(body, mesh=mesh, in_specs=in_specs, out_specs=out_specs, check_vma=False)
```

profile of v0, /device:TPU:65, one launch (start us, length us, event | category | flops | bytes accessed | tf_op | source)
XLA Modules:
  0.0 399.2 jit_solution(16000641626738499974)
XLA Ops:
  0.0 0.0 copy-start
  0.0 1.6 copy-done
  1.6 0.0 copy-start.1
  1.6 0.7 copy-done.1
  2.2 0.9 pick.1.outgoing
  3.1 81.3 %deal.1 = (f32[2,2048,128]{2,1,0:T(8,128)S(1)}, f32[256,256]{1,0:T(8,128)S(1)}, f32[2,1280,128]{2,1,0:T(8,128)S(1)}, f32[2,1280,128]{2,1,0:T(8,128)S(1)}) custom-call(f32[32,2,64,128]{3,2,1,0:T(8,128)S(1)} %pick.1.outgoing), custom_call_target="tpu_custom_call" | custom-call | tf_op jit(solution)/shard_map/deal/pallas_call | solution.py:741
  84.5 82.2 %rotation.3 = (f32[256,256]{1,0:T(8,128)S(1)}, f32[128,128]{1,0:T(8,128)S(1)}, f32[128,128]{1,0:T(8,128)S(1)}) custom-call(f32[256,256]{1,0:T(8,128)S(1)} %get-tuple-element.27.gram_ref), custom_call_target="tpu_custom_call" | custom-call | tf_op jit(solution)/shard_map/rotation/pallas_call | solution.py:124
  166.6 26.7 %next_round.2 = (f32[2,2048,128]{2,1,0:T(8,128)S(1)}, f32[256,256]{1,0:T(8,128)S(1)}, f32[2,768,128]{2,1,0:T(8,128)S(1)}, f32[2,768,128]{2,1,0:T(8,128)S(1)}) custom-call(f32[2,2048,128]{2,1,0:T(8,128)S(1)} %get-tuple-element.24.blocks, f32[2,1280,128]{2,1,0:T(8,128)S(1)} %get-tuple-element.25.before, f32[2,1280,128]{2,1,0:T(8,128)S(1)} %get-tuple-element.26.after, ...), custom_call_target="tpu_custom_call" | custom-call | tf_op jit(solution)/shard_map/next_round/pallas_call | solution.py:578
  193.4 82.3 %rotation.4 = (f32[256,256]{1,0:T(8,128)S(1)}, f32[128,128]{1,0:T(8,128)S(1)}, f32[128,128]{1,0:T(8,128)S(1)}) custom-call(f32[256,256]{1,0:T(8,128)S(1)} %get-tuple-element.34.gram_ref), custom_call_target="tpu_custom_call" | custom-call | tf_op jit(solution)/shard_map/rotation/pallas_call | solution.py:124
  275.7 27.0 %next_round.3 = (f32[2,2048,128]{2,1,0:T(8,128)S(1)}, f32[256,256]{1,0:T(8,128)S(1)}, f32[2,768,128]{2,1,0:T(8,128)S(1)}, f32[2,768,128]{2,1,0:T(8,128)S(1)}) custom-call(f32[2,2048,128]{2,1,0:T(8,128)S(1)} %get-tuple-element.31.blocks, f32[2,768,128]{2,1,0:T(8,128)S(1)} %get-tuple-element.32.before, f32[2,768,128]{2,1,0:T(8,128)S(1)} %get-tuple-element.33.after, ...), custom_call_target="tpu_custom_call" | custom-call | tf_op jit(solution)/shard_map/next_round/pallas_call | solution.py:578
  302.7 82.5 %rotation.5 = (f32[256,256]{1,0:T(8,128)S(1)}, f32[128,128]{1,0:T(8,128)}, f32[128,128]{1,0:T(8,128)}) custom-call(f32[256,256]{1,0:T(8,128)S(1)} %get-tuple-element.41.gram_ref), custom_call_target="tpu_custom_call" | custom-call | tf_op jit(solution)/shard_map/rotation/pallas_call | solution.py:124
  385.2 12.5 %last_round.1.blocks = f32[2,2048,128]{2,1,0:T(8,128)S(1)} custom-call(f32[2,2048,128]{2,1,0:T(8,128)S(1)} %get-tuple-element.38.blocks, f32[2,768,128]{2,1,0:T(8,128)S(1)} %get-tuple-element.39.before, f32[2,768,128]{2,1,0:T(8,128)S(1)} %get-tuple-element.40.after, f32[256,256]{1,0:T(8,128)S(1)} %get-tuple-element.42.rotation), custom_call_target="tpu_custom_call" | custom-call | tf_op jit(solution)/shard_map/last_round/pallas_call | solution.py:602
  397.7 1.4 join.1
Async XLA Ops:
  0.0 1.6 copy-start
  1.6 0.7 copy-start.1
where the time goes:
time: 402 us; the launch traced here: 399 us
  Pallas kernels  397 us (99%)
    pallas_call x3, Pallas kernels, make_rotation(): pl.pallas_call(functools.partial(rotation_kernel, total_rows), out_shape=...  247 us
    pallas_call x1, Pallas kernels, deal(): pl.pallas_call(functools.partial(deal_kernel, grid, cut), out_shape=(jax....  81.3 us
    pallas_call x2, Pallas kernels, next_round(): pl.pallas_call(functools.partial(round_kernel, grid, span), out_shape=(ja...  53.7 us
    pallas_call x1, Pallas kernels, last_round(): pl.pallas_call(last_kernel, out_shape=jax.ShapeDtypeStruct(blocks.shape,...  12.5 us

commit v1 on v0

--- a/solution.py
+++ b/solution.py
@@ -35,11 +35,19 @@
     eye = rows == cols
     above = rows < cols
 
+    small_eye = eye[:block, :block]
+
+    def diag(a, axis):
+        corners = (a[:block, :block], a[block:, block:])
+        return jnp.concatenate(
+            [jnp.sum(jnp.where(small_eye, corner, 0.0), axis=axis, keepdims=True) for corner in corners], axis=1 - axis
+        )
+
     def diag_row(a):
-        return jnp.sum(jnp.where(eye, a, 0.0), axis=0, keepdims=True)
+        return diag(a, 0)
 
     def diag_col(a):
-        return jnp.sum(jnp.where(eye, a, 0.0), axis=1, keepdims=True)
+        return diag(a, 1)
 
     current[...] = gram_ref[...]
     for sweep in range(SWEEPS):
@@ -52,8 +60,9 @@
         square = product(parts, parts)
         basis[...] = jnp.where(eye, 1.0, 0.0) + generator
         level[...] = 1.0 - diag_col(square)
-        strict[...] = jnp.where(above, -square, 0.0)
-        size = jnp.sum(square * square * jnp.where(above, 1.0, 0.0))
+        first_strict = jnp.where(above, -square, 0.0)
+        strict[...] = first_strict
+        size = jnp.sum(first_strict * first_strict)
 
         @pl.when(size > 0.0625)
         def _():
@@ -82,27 +91,25 @@
             _, count = state
             upper = strict[...]
             scale = level[...]
-            ratio = upper / scale
-            ratio_parts = halves(ratio)
+            ratio = upper * (1.0 / scale)
             turned = basis[...]
-            basis[...] = turned - product(halves(turned), ratio_parts)
-            size_now = jnp.sum(upper * upper)
-
-            @pl.when(size_now > 1e-06)
-            def _():
-                second = product(halves(upper), ratio_parts)
-                mixed = product(halves(ratio.T), halves(0.5 * upper - second))
-                level[...] = scale - 2.0 * diag_col(mixed)
-                strict[...] = jnp.where(above, -(second + mixed + mixed.T), 0.0)
-
-            return size_now, count + 1
+            both = product(halves(jnp.concatenate([turned, upper], axis=0)), halves(ratio))
+            basis[...] = turned - both[:width]
+            second = both[width:]
+            mixed = product(halves(ratio.T), halves(0.5 * upper - second))
+            level[...] = scale - 2.0 * diag_col(mixed)
+            left = jnp.where(above, -(second + mixed + mixed.T), 0.0)
+            strict[...] = left
+            return jnp.sum(left * left), count + 1
 
         lax.while_loop(
             lambda state: jnp.logical_and(state[0] > 1e-06, state[1] < width),
             eliminate,
-            (jnp.float32(1.0), jnp.int32(0)),
-        )
-        level_out = jnp.sum(jnp.where(eye, jnp.broadcast_to(level[...], (width, width)), 0.0), axis=0, keepdims=True)
+            (jnp.where(size > 0.0625, 0.0, size), jnp.int32(0)),
+        )
+        turned = basis[...]
+        basis[...] = turned - product(halves(turned), halves(strict[...] * (1.0 / level[...])))
+        level_out = diag_row(jnp.broadcast_to(level[...], (width, width)))
         step_rot = basis[...] * lax.rsqrt(level_out)
         step_parts = halves(step_rot)
         half = product(halves(current[...]), step_parts)
@@ -331,9 +338,10 @@
 
         lax.fori_loop(low, high, one, 0)
 
+    def begin():
+        start(0, pieces, jnp.logical_not(bent_on), jnp.logical_not(bent_back))
+
     def beside(phase):
-        if phase == 0:
-            start(0, pieces, jnp.logical_not(bent_on), jnp.logical_not(bent_back))
         start(cuts_at[phase], cuts_at[phase + 1], bent_on, bent_back)
 
     def finish():
@@ -344,11 +352,11 @@
 
         lax.fori_loop(0, pieces, one, 0)
 
-    return beside, finish
+    return begin, beside, finish
 
 
 def turn_and_move(
-    blocks, before, after, rotation, fresh, ahead, back, own_high, own_low, lent, got, got_high, got_low,
+    blocks, before, after, rotation, fresh, ahead, back, own_high, own_low, raw_high, raw_low, lent, got, got_high, got_low,
     send, recv, spin_send, spin_recv, first, last, position, count, use,
 ):
     block = blocks.shape[2]
@@ -408,12 +416,31 @@
         turn(c, 0)
         return leave(c, 0)
 
+    def split_there(c, _):
+        rows = chunk_rows(c)
+        for way, edge, raw in ((0, first, before), (1, last, after)):
+
+            @pl.when(edge)
+            def _(way=way):
+                high, low = pair_rows(blocks, c)
+                raw_high[way, rows, :] = high
+                raw_low[way, rows, :] = low
+
+            @pl.when(jnp.logical_not(edge))
+            def _(way=way, raw=raw):
+                high, low = pair_rows(raw, c)
+                raw_high[way, rows, :] = high
+                raw_low[way, rows, :] = low
+
+        return 0
+
     early = (chunks + there) // 2
     lax.fori_loop(there, early, turn, 0)
     met(count)
     both_ways(*spins(), first, last, lambda copy: copy.start())
     lax.fori_loop(there, early, leave, 0)
     lax.fori_loop(early, chunks, turn_and_leave, 0)
+    lax.fori_loop(0, there, split_there, 0)
     both_arrive(*spins(), first, last)
 
     for way, edge in ((0, first), (1, last)):
@@ -431,16 +458,9 @@
 
     def turn_there(c, _):
         rows = chunk_rows(c)
-        for way, edge, raw in ((0, first, before), (1, last, after)):
-
-            @pl.when(edge)
-            def _(way=way):
-                fresh[way, rows, :] = product(pair_rows(blocks, c), (got_high[way], got_low[way]))
-
-            @pl.when(jnp.logical_not(edge))
-            def _(way=way, raw=raw):
-                fresh[way, rows, :] = product(pair_rows(raw, c), (got_high[way], got_low[way]))
-
+        for way in range(2):
+            pair = raw_high[way, rows, :], raw_low[way, rows, :]
+            fresh[way, rows, :] = product(pair, (got_high[way], got_low[way]))
         use(c)
         return 0
 
@@ -480,7 +500,7 @@
 
 def round_kernel(
     grid, span, blocks, before, after, rotation, upper_gram, lower_gram, fresh, gram, next_before, next_after,
-    ahead, back, own_high, own_low, lent, got, got_high, got_low, send, recv, spin_send, spin_recv,
+    ahead, back, own_high, own_low, raw_high, raw_low, lent, got, got_high, got_low, send, recv, spin_send, spin_recv,
     ahead_gram, back_gram, gram_send, gram_recv, raw_send, raw_recv,
     part, total, slots, sums, sum_send, sum_recv,
 ):
@@ -506,7 +526,7 @@
         part[...] += product(halves(fresh[0, rows, :]), halves(fresh[1, rows, :]), ((0,), (0,)))
 
     take, finish = turn_and_move(
-        blocks, before, after, rotation, fresh, ahead, back, own_high, own_low, lent, got, got_high, got_low,
+        blocks, before, after, rotation, fresh, ahead, back, own_high, own_low, raw_high, raw_low, lent, got, got_high, got_low,
         send, recv, spin_send, spin_recv, first, last, position, count + len(across), cross,
     )
 
@@ -519,10 +539,11 @@
             position,
         )
 
-    beside, raws_finish = raw_moves(
+    begin, beside, raws_finish = raw_moves(
         fresh, next_before, next_after, raw_send, raw_recv, position, first, last, span
     )
     both_ways(*grams(), first, last, lambda copy: copy.start())
+    begin()
     take()
     row_total(grid, CROSS_STREAMS, part, total, slots, sums, sum_send, sum_recv, beside)
     gram[:block, block:] = total[...]
@@ -535,19 +556,19 @@
 
 def last_kernel(
     blocks, before, after, rotation, fresh,
-    ahead, back, own_high, own_low, lent, got, got_high, got_low, send, recv, spin_send, spin_recv,
+    ahead, back, own_high, own_low, raw_high, raw_low, lent, got, got_high, got_low, send, recv, spin_send, spin_recv,
 ):
     position, first, last, peers, count = pair_place()
     greet(peers)
     take, finish = turn_and_move(
-        blocks, before, after, rotation, fresh, ahead, back, own_high, own_low, lent, got, got_high, got_low,
+        blocks, before, after, rotation, fresh, ahead, back, own_high, own_low, raw_high, raw_low, lent, got, got_high, got_low,
         send, recv, spin_send, spin_recv, first, last, position, count, lambda c: None,
     )
     take()
     finish()
 
 
-def move_scratch(rows, block):
+def move_scratch(rows, block, there):
     width = 2 * block
     chunks = rows // CHUNK
     return [
@@ -555,6 +576,8 @@
         pltpu.VMEM((rows, block), F32),
         pltpu.VMEM((width, width), BF16),
         pltpu.VMEM((width, width), BF16),
+        pltpu.VMEM((2, there, width), BF16),
+        pltpu.VMEM((2, there, width), BF16),
         pltpu.VMEM((2, width, block), F32),
         pltpu.VMEM((2, width, block), F32),
         pltpu.VMEM((2, width, block), BF16),
@@ -585,7 +608,7 @@
         ),
         in_specs=[VMEM] * 6,
         out_specs=(VMEM,) * 4,
-        scratch_shapes=move_scratch(rows, block)
+        scratch_shapes=move_scratch(rows, block, before.shape[1])
         + [pltpu.VMEM((block, block), F32), pltpu.VMEM((block, block), F32)]
         + [pltpu.SemaphoreType.DMA((2,))] * 2
         + [pltpu.SemaphoreType.DMA((2, 2 * ROUND_AHEAD))] * 2
@@ -604,7 +627,7 @@
         out_shape=jax.ShapeDtypeStruct(blocks.shape, F32),
         in_specs=[VMEM] * 4,
         out_specs=VMEM,
-        scratch_shapes=move_scratch(rows, block),
+        scratch_shapes=move_scratch(rows, block, before.shape[1]),
         compiler_params=pltpu.CompilerParams(collective_id=1, has_side_effects=True, vmem_limit_bytes=GRANT),
         name="last_round",
     )(blocks, before, after, rotation)
@@ -636,7 +659,7 @@
 
 
 def deal_kernel(
-    grid, cut, outgoing, blocks, gram, before, after, send, recv, own, raw_send, raw_recv,
+    grid, cut, outgoing, blocks, gram, before, after, high_sum, side_sum, send, recv, own, raw_send, raw_recv,
     part, total, slots, sums, sum_send, sum_recv,
 ):
     tall, ring, cores = cut
@@ -690,7 +713,8 @@
     for near in range(1, group):
         copy_at(0, near).start()
     keep.wait()
-    part[...] = jnp.zeros_like(part)
+    high_sum[...] = jnp.zeros_like(high_sum)
+    side_sum[...] = jnp.zeros_like(side_sum)
 
     def add(order, _):
         far = far_of(order)
@@ -700,27 +724,32 @@
             def _(near=near):
                 copy_at(far, near).wait_recv()
 
+        pieces = []
         for there in range(tall):
             source = (there * ring + (turn - far + ring) % ring) * cores
             rows = pl.ds(pl.multiple_of(source * sub_rows, sub_rows * cores), sub_rows * cores)
-            high, low = halves(jnp.concatenate([blocks[0, rows, :], blocks[1, rows, :]], axis=1))
-
-            def one(x, y):
-                return lax.dot_general(x, y, (((0,), (0,)), ((), ())), preferred_element_type=F32)
-
-            main, side_part = one(high, high), one(high, low)
-            whole = main + (side_part + side_part.T)
-            part[:block, :] += whole[:block, :block]
-            part[block : 2 * block, :] += whole[:block, block:]
-            part[2 * block :, :] += whole[block:, block:]
+            pieces.append(jnp.concatenate([blocks[0, rows, :], blocks[1, rows, :]], axis=1))
+        high, low = halves(jnp.concatenate(pieces, axis=0))
+
+        def one(x, y):
+            return lax.dot_general(x, y, (((0,), (0,)), ((), ())), preferred_element_type=F32)
+
+        high_sum[...] += one(high, high)
+        side_sum[...] += one(high, low)
         return 0
 
     lax.fori_loop(0, ring, add, 0)
+    mixed = side_sum[...]
+    whole = high_sum[...] + (mixed + mixed.T)
+    part[:block, :] = whole[:block, :block]
+    part[block : 2 * block, :] = whole[:block, block:]
+    part[2 * block :, :] = whole[block:, block:]
     position, first, last, _, _ = pair_place()
 
-    beside, raws_finish = raw_moves(
+    begin, beside, raws_finish = raw_moves(
         blocks, before, after, raw_send, raw_recv, position, first, last, ring * cores
     )
+    begin()
     row_total(grid, GRAM_STREAMS, part, total, slots, sums, sum_send, sum_recv, beside)
     gram[:block, :block] = total[:block, :]
     gram[:block, block:] = total[block : 2 * block, :]
@@ -749,6 +778,8 @@
         in_specs=[VMEM],
         out_specs=(VMEM,) * 4,
         scratch_shapes=[
+            pltpu.VMEM((2 * block, 2 * block), F32),
+            pltpu.VMEM((2 * block, 2 * block), F32),
             pltpu.SemaphoreType.DMA((devices,)),
             pltpu.SemaphoreType.DMA((devices,)),
             pltpu.SemaphoreType.DMA,

time: 402 us -> 391 us (0.973)
  the two profiles are of different devices: /device:TPU:65 before, /device:TPU:393 now
where the time goes in v1:
time: 391 us; the launch traced here: 385 us
  Pallas kernels  382 us (98%)
    pallas_call x3, Pallas kernels, make_rotation(): pl.pallas_call(functools.partial(rotation_kernel, total_rows), out_shape=...  173 us
    pallas_call x1, Pallas kernels, last_round(): pl.pallas_call(last_kernel, out_shape=jax.ShapeDtypeStruct(blocks.shape,...  79.4 us
    pallas_call x1, Pallas kernels, deal(): pl.pallas_call(functools.partial(deal_kernel, grid, cut), out_shape=(jax....  75.3 us
    pallas_call x2, Pallas kernels, next_round(): pl.pallas_call(functools.partial(round_kernel, grid, span), out_shape=(ja...  52.4 us

profile of v1, /device:TPU:393, one launch (start us, length us, event | category | flops | bytes accessed | tf_op | source)
XLA Modules:
  0.0 384.9 jit_solution(6018463104663506299)
XLA Ops:
  0.0 0.0 copy-start
  0.0 1.6 copy-done
  1.6 0.0 copy-start.1
  1.6 0.7 copy-done.1
  2.2 0.9 pick.1.outgoing
  3.1 75.3 %deal.1 = (f32[2,2048,128]{2,1,0:T(8,128)S(1)}, f32[256,256]{1,0:T(8,128)S(1)}, f32[2,1280,128]{2,1,0:T(8,128)S(1)}, f32[2,1280,128]{2,1,0:T(8,128)S(1)}) custom-call(f32[32,2,64,128]{3,2,1,0:T(8,128)S(1)} %pick.1.outgoing), custom_call_target="tpu_custom_call" | custom-call | tf_op jit(solution)/shard_map/deal/pallas_call | solution.py:770
  78.4 82.3 %rotation.3 = (f32[256,256]{1,0:T(8,128)S(1)}, f32[128,128]{1,0:T(8,128)S(1)}, f32[128,128]{1,0:T(8,128)S(1)}) custom-call(f32[256,256]{1,0:T(8,128)S(1)} %get-tuple-element.27.gram_ref), custom_call_target="tpu_custom_call" | custom-call | tf_op jit(solution)/shard_map/rotation/pallas_call | solution.py:131
  160.7 26.1 %next_round.2 = (f32[2,2048,128]{2,1,0:T(8,128)S(1)}, f32[256,256]{1,0:T(8,128)S(1)}, f32[2,768,128]{2,1,0:T(8,128)S(1)}, f32[2,768,128]{2,1,0:T(8,128)S(1)}) custom-call(f32[2,2048,128]{2,1,0:T(8,128)S(1)} %get-tuple-element.24.blocks, f32[2,1280,128]{2,1,0:T(8,128)S(1)} %get-tuple-element.25.before, f32[2,1280,128]{2,1,0:T(8,128)S(1)} %get-tuple-element.26.after, ...), custom_call_target="tpu_custom_call" | custom-call | tf_op jit(solution)/shard_map/next_round/pallas_call | solution.py:601
  186.9 82.5 %rotation.4 = (f32[256,256]{1,0:T(8,128)S(1)}, f32[128,128]{1,0:T(8,128)S(1)}, f32[128,128]{1,0:T(8,128)S(1)}) custom-call(f32[256,256]{1,0:T(8,128)S(1)} %get-tuple-element.34.gram_ref), custom_call_target="tpu_custom_call" | custom-call | tf_op jit(solution)/shard_map/rotation/pallas_call | solution.py:131
  269.3 26.3 %next_round.3 = (f32[2,2048,128]{2,1,0:T(8,128)S(1)}, f32[256,256]{1,0:T(8,128)S(1)}, f32[2,768,128]{2,1,0:T(8,128)S(1)}, f32[2,768,128]{2,1,0:T(8,128)S(1)}) custom-call(f32[2,2048,128]{2,1,0:T(8,128)S(1)} %get-tuple-element.31.blocks, f32[2,768,128]{2,1,0:T(8,128)S(1)} %get-tuple-element.32.before, f32[2,768,128]{2,1,0:T(8,128)S(1)} %get-tuple-element.33.after, ...), custom_call_target="tpu_custom_call" | custom-call | tf_op jit(solution)/shard_map/next_round/pallas_call | solution.py:601
  295.6 8.3 %rotation.5 = (f32[256,256]{1,0:T(8,128)S(1)}, f32[128,128]{1,0:T(8,128)}, f32[128,128]{1,0:T(8,128)}) custom-call(f32[256,256]{1,0:T(8,128)S(1)} %get-tuple-element.41.gram_ref), custom_call_target="tpu_custom_call" | custom-call | tf_op jit(solution)/shard_map/rotation/pallas_call | solution.py:131
  303.9 79.4 %last_round.1.blocks = f32[2,2048,128]{2,1,0:T(8,128)S(1)} custom-call(f32[2,2048,128]{2,1,0:T(8,128)S(1)} %get-tuple-element.38.blocks, f32[2,768,128]{2,1,0:T(8,128)S(1)} %get-tuple-element.39.before, f32[2,768,128]{2,1,0:T(8,128)S(1)} %get-tuple-element.40.after, f32[256,256]{1,0:T(8,128)S(1)} %get-tuple-element.42.rotation), custom_call_target="tpu_custom_call" | custom-call | tf_op jit(solution)/shard_map/last_round/pallas_call | solution.py:625
  383.4 1.4 join.1
Async XLA Ops:
  0.0 1.6 copy-start
  1.6 0.7 copy-start.1
